TPU v7x, 32 devices: a whole 2x2x4 slice. The times are simulated.
32 devices in a mesh: parts: 1, seq: 32 (over z, y, x, core).
Axes of the slice: x: 2, y: 2, z: 4, core: 2. Of those that a mesh axis runs over, the one named last changes fastest.
Arguments:
- tokens: bfloat16 [1, 128, 3, 128, 3072], P('parts', 'seq'), may hold values from -6 to 6
- queries: bfloat16 [1, 128, 3, 128, 1536], P('parts', 'seq'), may hold values from -68 to 68
- key_weight: bfloat16 [3072, 1536], P('seq'), may hold values from -0.109375 to 0.109375
- value_weight: bfloat16 [3072, 1536], P('seq'), may hold values from -0.109375 to 0.109375
- halves: int32 [1, 128, 3, 2, 2], P('parts', 'seq'), may hold values from 1 to 3
Outputs:
- mixed: bfloat16 [1, 128, 3, 128, 1536], P('parts', 'seq')
Inputs may be any that keep to these rules, and one draw needn't show every extreme that they name: `halves`: 1 lists the first half of the partner lines, 2 the second half, 3 both.
All inputs are finite; a program needn't handle non-finite values.
Results may differ from a plain program's by a relative error of at most 0.012.
Values may be sent and summed in bfloat16 or wider, within the bound.
No kernel may reach another device: no remote copies, remote signals or barrier semaphores. Data moves between devices by JAX's collectives and lax.ppermute only.
A program may use at most 128 MiB of HBM per device.

v0:
```python
import math
import jax
import jax.numpy as jnp
from jax import lax
from jax.sharding import PartitionSpec as P

HEADS = 12
HDIM = 128


def split_heads(tensor_in):
    return tensor_in.reshape(tensor_in.shape[:-1] + (HEADS, HDIM))


def kept_keys(code_grid, grid_len):
    column = jnp.arange(grid_len)
    first_kept = (code_grid % 2 == 1)[..., None]
    second_kept = (code_grid >= 2)[..., None]
    return jnp.where(column < grid_len // 2, first_kept, second_kept)[..., None, :]


def codes_by_half(code_pairs, half_index):
    return jnp.where(half_index[None, None, :] == 0, code_pairs[..., 0:1], code_pairs[..., 1:2])


def partial_attention(queries_h, keys_h, values_h, score_form, value_form, kept_mask):
    scores = jnp.einsum(score_form, queries_h, keys_h, preferred_element_type=jnp.float32) * (
        1.0 / math.sqrt(HDIM)
    )
    masked = jnp.where(kept_mask, scores, -jnp.inf)
    peak_val = jnp.max(masked, axis=-1)
    weights = jnp.exp(masked - peak_val[..., None])
    totals = jnp.sum(weights, axis=-1)
    partial_out = jnp.einsum(
        value_form, weights.astype(jnp.bfloat16), values_h, preferred_element_type=jnp.float32
    )
    return (partial_out, peak_val, totals)


def merge_slots(near_part, far_part):
    peak_val = jnp.maximum(near_part[1], far_part[1])
    near_w = jnp.exp(near_part[1] - peak_val)
    far_w = jnp.exp(far_part[1] - peak_val) * far_part[2]
    upper = near_part[0] * near_w[..., None] + far_part[0] * far_w[..., None]
    return upper / (near_part[2] * near_w + far_w)[..., None]


def on_device(tokens, queries, key_weight, value_weight, halves):
    scenes, line_count, planes, grid_len, model_width = tokens.shape
    hidden_width = queries.shape[-1]
    home_rows = tokens.reshape(-1, model_width)

    def add_panel(weight_panel):
        return jnp.dot(home_rows, weight_panel, preferred_element_type=jnp.float32)

    key_sum = add_panel(lax.all_gather(key_weight, "seq", axis=0, tiled=True))
    value_sum = add_panel(lax.all_gather(value_weight, "seq", axis=0, tiled=True))
    home_shape = (scenes, line_count, planes, grid_len, hidden_width)
    keys_home = key_sum.astype(jnp.bfloat16).reshape(home_shape)
    values_home = value_sum.astype(jnp.bfloat16).reshape(home_shape)
    moved_q, moved_k, moved_v = (
        lax.all_to_all(queries, "seq", split_axis=3, concat_axis=1, tiled=True),
        lax.all_to_all(keys_home, "seq", split_axis=3, concat_axis=1, tiled=True),
        lax.all_to_all(values_home, "seq", split_axis=3, concat_axis=1, tiled=True),
    )
    code_table = lax.all_gather(halves, "seq", axis=1, tiled=True)
    half_len = grid_len // 2
    own_start = lax.axis_index("seq") * line_count
    moved_half = (own_start + jnp.arange(line_count)) // half_len
    home_half = jnp.arange(grid_len) // half_len
    remote_plan = (
        (0, keys_home[:, :, 2], values_home[:, :, 2], "sabhd,sbjhd->sabhj", "sabhj,sbjhd->sabhd"),
        (1, moved_k[:, :, 2], moved_v[:, :, 2], "sabhd,sjbhd->sabhj", "sabhj,sjbhd->sabhd"),
        (2, moved_k[:, :, 1], moved_v[:, :, 1], "sabhd,sjbhd->sabhj", "sabhj,sjbhd->sabhd"),
    )
    remote_results = []
    for plane_idx, keys_part, values_part, score_form, value_form in remote_plan:
        code_grid = codes_by_half(code_table[:, :, plane_idx, :, 1], moved_half)
        remote_results.append(
            partial_attention(
                split_heads(moved_q[:, :, plane_idx]),
                split_heads(keys_part),
                split_heads(values_part),
                score_form,
                value_form,
                kept_keys(code_grid, grid_len),
            )
        )
    remote_mean = jnp.stack([result[0] / result[2][..., None] for result in remote_results], axis=2)
    remote_mean = remote_mean.reshape(remote_mean.shape[:4] + (hidden_width,)).astype(jnp.bfloat16)
    remote_peak = jnp.stack([result[1] for result in remote_results], axis=2)
    remote_sum = jnp.stack([result[2] for result in remote_results], axis=2)
    back_mean = lax.all_to_all(remote_mean, "seq", split_axis=1, concat_axis=3, tiled=True)
    back_peak, back_sum = (
        lax.all_to_all(remote_peak, "seq", split_axis=1, concat_axis=3, tiled=True),
        lax.all_to_all(remote_sum, "seq", split_axis=1, concat_axis=3, tiled=True),
    )
    home_plan = (
        (0, keys_home[:, :, 1], values_home[:, :, 1], "sabhd,sajhd->sabhj", "sabhj,sajhd->sabhd"),
        (1, keys_home[:, :, 0], values_home[:, :, 0], "sabhd,sajhd->sabhj", "sabhj,sajhd->sabhd"),
        (2, moved_k[:, :, 0], moved_v[:, :, 0], "sabhd,sjahd->sabhj", "sabhj,sjahd->sabhd"),
    )
    home_results = []
    for plane_idx, keys_part, values_part, score_form, value_form in home_plan:
        code_grid = codes_by_half(halves[:, :, plane_idx, :, 0], home_half)
        home_results.append(
            partial_attention(
                split_heads(queries[:, :, plane_idx]),
                split_heads(keys_part),
                split_heads(values_part),
                score_form,
                value_form,
                kept_keys(code_grid, grid_len),
            )
        )
    home_out = jnp.stack([result[0] for result in home_results], axis=2)
    home_peak = jnp.stack([result[1] for result in home_results], axis=2)
    home_sum = jnp.stack([result[2] for result in home_results], axis=2)
    merged = merge_slots(
        (home_out, home_peak, home_sum),
        (split_heads(back_mean.astype(jnp.float32)), back_peak, back_sum),
    )
    return merged.reshape(home_shape).astype(jnp.bfloat16)


def solution(mesh):
    in_specs = (
        P("parts", "seq", None, None, None),
        P("parts", "seq", None, None, None),
        P("seq", None),
        P("seq", None),
        P("parts", "seq", None, None, None),
    )
    out_specs = P("parts", "seq", None, None, None)
    return jax.shard_map(
        on_device, mesh=mesh, in_specs=in_specs, out_specs=out_specs, check_vma=False
    )
```

profile of v0, /device:TPU:0, one launch (start us, length us, event | category | flops | bytes accessed | tf_op | source)
XLA Modules:
  0.0 732.5 jit_solution(9357103538851799629)
XLA Ops:
  8.0 8.2 %copy.418 = bf16[1,4,3,128,1536]{4,1,2,0,3:T(4,128)(2,1)} copy(bf16[1,4,3,128,1536]{4,3,2,1,0:T(8,128)(2,1)} %param.6) | data formatting | bytes 9437184 | tf_op args[1]
  16.2 7.4 %all-to-all-start.2 = ((bf16[1,4,3,128,1536]{4,1,2,0,3:T(4,128)(2,1)}), bf16[1,4,3,128,1536]{4,1,2,0,3:T(4,128)(2,1)}, u32[]{:S(2)}, u32[]{:S(2)}) async-start(bf16[1,4,3,128,1536]{4,1,2,0,3:T(4,128)(2,1)} %copy.418), calls=%async_computation.2 | async-start | bytes 9437184 | tf_op jit(solution)/shard_map/all_to_all | solution.py:62
  23.6 128.7 %all-gather.3.cloned.1.call-done = bf16[3072,1536]{1,0:T(8,128)(2,1)} async-done(((bf16[96,1536]{1,0:T(8,128)(2,1)}), bf16[3072,1536]{1,0:T(8,128)(2,1)}) %all-gather.3.cloned.1.call-update) | async-done | bytes 9437200 | tf_op jit(solution)/shard_map/all_gather | solution.py:57
  152.3 19.9 %convolution_convert_fusion.1 = bf16[1536,1536]{1,0:T(8,128)(2,1)S(1)} fusion(bf16[1536,3072]{1,0:T(8,128)(2,1)} %bitcast.326, bf16[3072,1536]{1,0:T(8,128)(2,1)} %all-gather.3.cloned.1.call-done), kind=kOutput, calls=%fused_computation.7 | convolution fusion | flops 14497873920 | bytes 23592960 | tf_op jit(solution)/shard_map/dot_general | solution.py:54
  174.3 5.8 copy.400
  184.0 105.3 %all-gather.5.cloned.1.call-done = bf16[3072,1536]{1,0:T(8,128)(2,1)} async-done(((bf16[96,1536]{1,0:T(8,128)(2,1)}), bf16[3072,1536]{1,0:T(8,128)(2,1)}) %all-gather.5.cloned.1.call-update) | async-done | bytes 9437200 | tf_op jit(solution)/shard_map/all_gather | solution.py:56
  289.3 19.9 %convolution_convert_fusion = bf16[1536,1536]{1,0:T(8,128)(2,1)S(1)} fusion(bf16[1536,3072]{1,0:T(8,128)(2,1)} %bitcast.327, bf16[3072,1536]{1,0:T(8,128)(2,1)} %all-gather.5.cloned.1.call-done), kind=kOutput, calls=%fused_computation.6 | convolution fusion | flops 14497873920 | bytes 23592960 | tf_op jit(solution)/shard_map/dot_general | solution.py:54
  311.4 5.8 copy.404
  317.2 7.0 all-to-all-done
  328.1 113.8 %all_gather.11 = s32[1,128,3,2,2]{2,4,3,0,1:T(2,128)S(1)} all-gather(s32[1,4,3,2,2]{2,4,3,0,1:T(2,128)S(1)} %copy.415), channel_id=1, replica_groups=mesh['parts'=1,'seq'=32] {'seq'}, dimensions={1}, use_global_device_ids=true | all-gather | bytes 6336 | tf_op jit(solution)/shard_map/all_gather | solution.py:66
  443.1 4.7 copy.419
  459.9 4.4 fusion.97
  465.9 4.5 fusion.96
  519.5 19.8 %all-to-all-start.3 = ((f32[32,1,576]{2,1,0:T(1,128)}), f32[32,1,576]{2,1,0:T(1,128)S(1)}, u32[]{:S(2)}, u32[]{:S(2)}) async-start(f32[32,1,576]{2,1,0:T(1,128)} %reshape.1497), calls=%async_computation.3 | async-start | bytes 163840 | tf_op jit(solution)/shard_map/all_to_all | solution.py:95
  554.8 5.9 all-to-all-start.5
  560.8 6.4 pad_maximum_fusion
  569.0 4.8 all-to-all-start.4
  605.9 4.2 copy.407
  635.6 43.3 %all-to-all-done.4 = bf16[1,128,3,4,1536]{4,3,2,0,1:T(4,128)(2,1)} async-done(((bf16[1,128,3,4,1536]{4,3,2,0,1:T(4,128)(2,1)}), bf16[1,128,3,4,1536]{4,3,2,0,1:T(4,128)(2,1)}, u32[]{:S(2)}, u32[]{:S(2)}) %all-to-all-start.4) | async-done | bytes 4718624 | tf_op jit(solution)/shard_map/all_to_all | solution.py:93
  678.9 7.4 %convert_bitcast_fusion = f32[1,4,3,32,4,1536]{5,4,2,1,3,0:T(4,128)} fusion(bf16[1,32,4,3,4,1536]{5,4,3,2,1,0:T(4,128)(2,1)} %bitcast.133), kind=kLoop, calls=%fused_computation.3 | loop fusion | flops 2359296 | bytes 14155776 | tf_op jit(solution)/shard_map/convert_element_type | solution.py:121
  686.3 11.8 %copy.447 = f32[1,4,3,32,4,1536]{5,1,4,3,2,0:T(4,128)} copy(f32[1,4,3,32,4,1536]{5,4,2,1,3,0:T(4,128)} %convert_bitcast_fusion) | data formatting | bytes 18874368 | tf_op jit(solution)/shard_map/convert_element_type | solution.py:121
  698.1 12.0 %copy.454 = f32[1,4,3,128,1536]{3,4,2,1,0:T(8,128)} copy(f32[1,4,3,128,1536]{4,1,3,2,0:T(4,128)} %bitcast.266) | data formatting | bytes 18874368 | tf_op jit(solution)/shard_map/convert_element_type | solution.py:121
  710.1 8.8 %fusion.2 = bf16[1,4,3,128,1536]{3,4,2,1,0:T(8,128)(2,1)} fusion(f32[1,4,3,128,1536]{3,4,2,1,0:T(8,128)} %copy.454, f32[1,4,1,128,1536]{3,4,2,1,0:T(8,128)} %bitcast.278, f32[1,4,1,128,1536]{3,4,2,1,0:T(8,128)} %bitcast.277, f32[1,4,1,128,1536]{3,4,2,1,0:T(8,128)S(1)} %bitcast.276, f32[4,3,128,12]{2,3,0,1:T(8,128)S(1)} %get-tuple-element.6, ...), kind=kLoop, calls=%fused_computation.5 | loop fusion | flops 16515072 | bytes 23814144 | tf_op jit(solution)/shard_map/convert_element_type | solution.py:123
  718.9 6.6 copy.456
  (157 shorter events, 151.9 us)
Async XLA Ops:
  6.5 145.7 %all-gather.3.cloned.1.call-start = ((), (), s32[]{:S(2)}) async-start(), calls=%async_computation.6 | async-start | bytes 9732096 | tf_op jit(solution)/shard_map/all_gather | solution.py:57
  7.3 282.0 %all-gather.5.cloned.1.call-start = ((), (), s32[]{:S(2)}) async-start(), calls=%async_computation.7 | async-start | bytes 9732096 | tf_op jit(solution)/shard_map/all_gather | solution.py:56
  16.2 164.0 %all-to-all-start.2 = ((bf16[1,4,3,128,1536]{4,1,2,0,3:T(4,128)(2,1)}), bf16[1,4,3,128,1536]{4,1,2,0,3:T(4,128)(2,1)}, u32[]{:S(2)}, u32[]{:S(2)}) async-start(bf16[1,4,3,128,1536]{4,1,2,0,3:T(4,128)(2,1)} %copy.418), calls=%async_computation.2 | async-start | bytes 9437184 | tf_op jit(solution)/shard_map/all_to_all | solution.py:62
  180.2 144.1 %all-to-all-start = ((bf16[1,4,3,128,1536]{4,1,2,0,3:T(4,128)(2,1)}), bf16[1,4,3,128,1536]{4,1,2,0,3:T(4,128)(2,1)}, u32[]{:S(2)}, u32[]{:S(2)}) async-start(bf16[1,4,3,128,1536]{4,1,2,0,3:T(4,128)(2,1)} %copy.400), calls=%async_computation | async-start | bytes 9437184 | tf_op jit(solution)/shard_map/all_to_all | solution.py:64
  317.2 10.8 %copy-start.29 = (s32[1,4,3,2,2]{1,4,3,2,0:T(2,128)S(1)}, s32[1,4,3,2,2]{1,4,3,2,0:T(2,128)}, u32[]{:S(2)}) copy-start(s32[1,4,3,2,2]{1,4,3,2,0:T(2,128)} %param.9) | copy-start | bytes 580
  324.2 169.1 %all-to-all-start.1 = ((bf16[1,4,3,128,1536]{4,1,2,0,3:T(4,128)(2,1)}), bf16[1,4,3,128,1536]{4,1,2,0,3:T(4,128)(2,1)}, u32[]{:S(2)}, u32[]{:S(2)}) async-start(bf16[1,4,3,128,1536]{4,1,2,0,3:T(4,128)(2,1)} %copy.404), calls=%async_computation.1 | async-start | bytes 9437184 | tf_op jit(solution)/shard_map/all_to_all | solution.py:63
  442.8 5.0 copy-start.31
  519.5 35.3 %all-to-all-start.3 = ((f32[32,1,576]{2,1,0:T(1,128)}), f32[32,1,576]{2,1,0:T(1,128)S(1)}, u32[]{:S(2)}, u32[]{:S(2)}) async-start(f32[32,1,576]{2,1,0:T(1,128)} %reshape.1497), calls=%async_computation.3 | async-start | bytes 163840 | tf_op jit(solution)/shard_map/all_to_all | solution.py:95
  539.3 3.9 copy-start.3
  539.3 3.9 copy-start.17
  545.6 5.4 copy-start.24
  545.6 5.4 copy-start.25
  546.9 13.9 %copy-start.7 = (bf16[1,128,1,4,1536]{4,3,2,0,1:T(4,128)(2,1)S(1)}, bf16[1,128,1,4,1536]{4,3,2,0,1:T(4,128)(2,1)}, u32[]{:S(2)}) copy-start(bf16[1,128,1,4,1536]{4,3,2,0,1:T(4,128)(2,1)} %copy.444) | copy-start | bytes 4718596
  554.8 13.5 %all-to-all-start.5 = ((f32[32,1,576]{2,1,0:T(1,128)}), f32[32,1,576]{2,1,0:T(1,128)S(1)}, u32[]{:S(2)}, u32[]{:S(2)}) async-start(f32[32,1,576]{2,1,0:T(1,128)} %reshape.1495), calls=%async_computation.5 | async-start | bytes 163840 | tf_op jit(solution)/shard_map/all_to_all | solution.py:96
  569.0 109.9 %all-to-all-start.4 = ((bf16[1,128,3,4,1536]{4,3,2,0,1:T(4,128)(2,1)}), bf16[1,128,3,4,1536]{4,3,2,0,1:T(4,128)(2,1)}, u32[]{:S(2)}, u32[]{:S(2)}) async-start(bf16[1,128,3,4,1536]{4,3,2,0,1:T(4,128)(2,1)} %pad_maximum_fusion), calls=%async_computation.4 | async-start | bytes 9437184 | tf_op jit(solution)/shard_map/all_to_all | solution.py:93
  579.4 4.3 copy-start.30
  579.4 4.5 copy-start.32
  579.4 4.6 copy-start.5
  581.0 4.7 copy-start.4
  585.7 4.3 copy-start.6
  587.3 4.3 copy-start.10
  624.4 9.5 %copy-start.27 = (f32[4,128,12]{1,2,0:T(8,128)S(1)}, f32[4,128,12]{1,2,0:T(8,128)}, u32[]{:S(2)}) copy-start(f32[4,128,12]{1,2,0:T(8,128)} %fusion.8) | copy-start | bytes 73732
  624.4 9.5 %copy-start.28 = (f32[4,128,12]{1,2,0:T(8,128)S(1)}, f32[4,128,12]{1,2,0:T(8,128)}, u32[]{:S(2)}) copy-start(f32[4,128,12]{1,2,0:T(8,128)} %fusion.10) | copy-start | bytes 73732
  698.1 12.0 %copy-start.20 = (f32[4,3,128,12]{2,3,0,1:T(8,128)S(1)}, f32[4,3,128,12]{2,3,0,1:T(8,128)}, u32[]{:S(2)}) copy-start(f32[4,3,128,12]{2,3,0,1:T(8,128)} %get-tuple-element.7) | copy-start | bytes 221188
  (17 other events, 31.8 us)
Sparse Core Ops, SparseCore 0:
  10.2 141.9 all-gather.2
  155.2 134.0 all-gather.4
where the time goes:
time: 743 us; the launch traced here: 733 us
  waiting for transfers between devices  287 us (39%)
  local copies, waits for them, and re-layouts  173 us (23%)
  blocking collectives  114 us (15%)
  matrix products  64.8 us (9%)
  starting transfers between devices  45.5 us (6%)
  other arithmetic  34.7 us (5%)
  between operations  14.1 us (2%)
    all_gather x1, waiting for transfers between devices, on_device(): lax.all_gather(value_weight, 'seq', axis=0, tiled=True)  129 us
    all_gather x1, blocking collectives, on_device(): code_table = lax.all_gather(halves, 'seq', axis=1, tiled=True)  114 us
    all_gather x1, waiting for transfers between devices, on_device(): key_sum = add_panel(lax.all_gather(key_weight, 'seq', axis=0, tiled=True))  105 us
    all_to_all x1, waiting for transfers between devices, on_device(): lax.all_to_all(remote_mean, 'seq', split_axis=1, concat_axis=3, tiled=True)  43.3 us
    dot_general x2, matrix products, add_panel(): return jnp.dot(home_rows, weight_panel, preferred_element_type=jnp.float32)  39.8 us
    unnamed x78, local copies, waits for them, and re-layouts  39.1 us
    convert_element_type x2, local copies, waits for them, and re-layouts, on_device(): back_mean.astype(jnp.float32)  23.8 us
    all_to_all x1, starting transfers between devices, on_device(): lax.all_to_all(remote_peak, 'seq', split_axis=1, concat_axis=3, tiled=True)  19.8 us
  transfers between devices with their start and end apart: 8, of which 5 were waited for; matrix products, arithmetic and copies ran while one was open for 26% of the time, Pallas kernels for 0%

commit v1 on v0

--- a/solution.py
+++ b/solution.py
@@ -90,7 +90,9 @@
     remote_mean = remote_mean.reshape(remote_mean.shape[:4] + (hidden_width,)).astype(jnp.bfloat16)
     remote_peak = jnp.stack([result[1] for result in remote_results], axis=2)
     remote_sum = jnp.stack([result[2] for result in remote_results], axis=2)
-    back_mean = lax.all_to_all(remote_mean, "seq", split_axis=1, concat_axis=3, tiled=True)
+    shards = jnp.split(remote_mean, lax.axis_size("seq"), axis=1)
+    received = lax.all_to_all(jnp.stack(shards), "seq", 0, 0)
+    back_mean = jnp.concatenate(received, axis=3)
     back_peak, back_sum = (
         lax.all_to_all(remote_peak, "seq", split_axis=1, concat_axis=3, tiled=True),
         lax.all_to_all(remote_sum, "seq", split_axis=1, concat_axis=3, tiled=True),

time: 743 us -> 755 us (1.016)
  local copies, waits for them, and re-layouts: 173 us -> 186 us
    unnamed x78 -> x83, local copies, waits for them, and re-layouts: 39.1 us -> 45.5 us
  transfers between devices with their start and end apart: 8 -> 8, of which waited for: 5 -> 5; matrix products, arithmetic and copies ran while one was open for 26% -> 25% of each run, Pallas kernels for 0% -> 0%
where the time goes in v1:
time: 755 us; the launch traced here: 744 us
  waiting for transfers between devices  290 us (38%)
  local copies, waits for them, and re-layouts  186 us (25%)
  blocking collectives  114 us (15%)
  matrix products  66.7 us (9%)
  starting transfers between devices  43.9 us (6%)
  other arithmetic  29.5 us (4%)
  between operations  14.3 us (2%)
    all_gather x1, waiting for transfers between devices, on_device(): lax.all_gather(value_weight, 'seq', axis=0, tiled=True)  129 us
    all_gather x1, blocking collectives, on_device(): code_table = lax.all_gather(halves, 'seq', axis=1, tiled=True)  114 us
    all_gather x1, waiting for transfers between devices, on_device(): key_sum = add_panel(lax.all_gather(key_weight, 'seq', axis=0, tiled=True))  105 us
    unnamed x83, local copies, waits for them, and re-layouts  45.5 us
    all_to_all x1, waiting for transfers between devices, on_device(): received = lax.all_to_all(jnp.stack(shards), 'seq', 0, 0)  41.5 us
    dot_general x2, matrix products, add_panel(): return jnp.dot(home_rows, weight_panel, preferred_element_type=jnp.float32)  39.8 us
    convert_element_type x2, local copies, waits for them, and re-layouts, on_device(): back_mean.astype(jnp.float32)  22.5 us
    all_to_all x1, starting transfers between devices, on_device(): lax.all_to_all(remote_peak, 'seq', split_axis=1, concat_axis=3, tiled=True)  19.6 us
  transfers between devices with their start and end apart: 8, of which 5 were waited for; matrix products, arithmetic and copies ran while one was open for 25% of the time, Pallas kernels for 0%

profile of v1, /device:TPU:0, one launch (start us, length us, event | category | flops | bytes accessed | tf_op | source)
XLA Modules:
  0.0 744.3 jit_solution(7172693686559763132)
XLA Ops:
  8.0 8.2 %copy.445 = bf16[1,4,3,128,1536]{4,1,2,0,3:T(4,128)(2,1)} copy(bf16[1,4,3,128,1536]{4,3,2,1,0:T(8,128)(2,1)} %param.6) | data formatting | bytes 9437184 | tf_op args[1]
  16.2 7.4 all-to-all-start.2
  23.6 128.6 %all-gather.3.cloned.1.call-done = bf16[3072,1536]{1,0:T(8,128)(2,1)} async-done(((bf16[96,1536]{1,0:T(8,128)(2,1)}), bf16[3072,1536]{1,0:T(8,128)(2,1)}) %all-gather.3.cloned.1.call-update) | async-done | bytes 9437200 | tf_op jit(solution)/shard_map/all_gather | solution.py:57
  152.2 19.9 %convolution_convert_fusion.1 = bf16[1536,1536]{1,0:T(8,128)(2,1)S(1)} fusion(bf16[1536,3072]{1,0:T(8,128)(2,1)} %bitcast.452, bf16[3072,1536]{1,0:T(8,128)(2,1)} %all-gather.3.cloned.1.call-done), kind=kOutput, calls=%fused_computation.7 | convolution fusion | flops 14497873920 | bytes 23592960 | tf_op jit(solution)/shard_map/dot_general | solution.py:54
  174.3 5.8 copy.427
  183.9 105.3 %all-gather.5.cloned.1.call-done = bf16[3072,1536]{1,0:T(8,128)(2,1)} async-done(((bf16[96,1536]{1,0:T(8,128)(2,1)}), bf16[3072,1536]{1,0:T(8,128)(2,1)}) %all-gather.5.cloned.1.call-update) | async-done | bytes 9437200 | tf_op jit(solution)/shard_map/all_gather | solution.py:56
  289.2 19.9 %convolution_convert_fusion = bf16[1536,1536]{1,0:T(8,128)(2,1)S(1)} fusion(bf16[1536,3072]{1,0:T(8,128)(2,1)} %bitcast.453, bf16[3072,1536]{1,0:T(8,128)(2,1)} %all-gather.5.cloned.1.call-done), kind=kOutput, calls=%fused_computation.6 | convolution fusion | flops 14497873920 | bytes 23592960 | tf_op jit(solution)/shard_map/dot_general | solution.py:54
  311.4 5.8 copy.431
  317.2 7.0 all-to-all-done
  328.0 113.8 %all_gather.11 = s32[1,128,3,2,2]{2,4,3,0,1:T(2,128)S(1)} all-gather(s32[1,4,3,2,2]{2,4,3,0,1:T(2,128)S(1)} %copy.442), channel_id=1, replica_groups=mesh['parts'=1,'seq'=32] {'seq'}, dimensions={1}, use_global_device_ids=true | all-gather | bytes 6336 | tf_op jit(solution)/shard_map/all_gather | solution.py:66
  443.1 4.7 copy.446
  466.4 4.6 fusion.128
  495.5 4.0 copy.467
  538.2 19.6 %all-to-all-start.3 = ((f32[32,1,576]{2,1,0:T(1,128)}), f32[32,1,576]{2,1,0:T(1,128)S(1)}, u32[]{:S(2)}, u32[]{:S(2)}) async-start(f32[32,1,576]{2,1,0:T(1,128)} %reshape.1496), calls=%async_computation.3 | async-start | bytes 163840 | tf_op jit(solution)/shard_map/all_to_all | solution.py:97
  568.9 5.8 all-to-all-start.5
  576.4 5.9 all-to-all-done.5
  586.5 4.6 fusion.127
  621.0 4.1 copy.434
  650.2 41.5 %all-to-all-done.4 = bf16[32,1,4,3,4,1536]{5,2,4,3,1,0:T(4,128)(2,1)} async-done(((bf16[32,1,4,3,4,1536]{5,2,4,3,1,0:T(4,128)(2,1)}), bf16[32,1,4,3,4,1536]{5,2,4,3,1,0:T(4,128)(2,1)}, u32[]{:S(2)}, u32[]{:S(2)}) %all-to-all-start.4) | async-done | bytes 4718624 | tf_op jit(solution)/shard_map/all_to_all | solution.py:94
  691.7 7.5 %convert_bitcast_fusion = f32[1,4,3,32,4,1536]{5,1,4,2,0,3:T(4,128)} fusion(bf16[32,1,4,3,4,1536]{5,2,4,3,1,0:T(4,128)(2,1)} %all-to-all-done.4), kind=kLoop, calls=%fused_computation.4 | loop fusion | flops 2359296 | bytes 14155776 | tf_op jit(solution)/shard_map/convert_element_type | solution.py:123
  699.1 10.4 %copy.474 = f32[1,4,3,32,4,1536]{5,1,4,3,2,0:T(4,128)} copy(f32[1,4,3,32,4,1536]{5,1,4,2,0,3:T(4,128)} %convert_bitcast_fusion) | data formatting | bytes 18874368 | tf_op jit(solution)/shard_map/convert_element_type | solution.py:123
  709.6 12.0 %copy.481 = f32[1,4,3,128,1536]{3,4,2,1,0:T(8,128)} copy(f32[1,4,3,128,1536]{4,1,3,2,0:T(4,128)} %bitcast.392) | data formatting | bytes 18874368 | tf_op jit(solution)/shard_map/convert_element_type | solution.py:123
  721.6 8.8 %fusion.2 = bf16[1,4,3,128,1536]{3,4,2,1,0:T(8,128)(2,1)} fusion(f32[1,4,3,128,1536]{3,4,2,1,0:T(8,128)} %copy.481, f32[1,4,1,128,1536]{3,4,2,1,0:T(8,128)} %bitcast.404, f32[1,4,1,128,1536]{3,4,2,1,0:T(8,128)} %bitcast.403, f32[1,4,1,128,1536]{3,4,2,1,0:T(8,128)S(1)} %bitcast.402, f32[4,3,128,12]{2,3,0,1:T(8,128)S(1)} %get-tuple-element.6, ...), kind=kLoop, calls=%fused_computation.5 | loop fusion | flops 16515072 | bytes 23814144 | tf_op jit(solution)/shard_map/convert_element_type | solution.py:125
  730.4 6.6 copy.483
  (163 shorter events, 168.0 us)
Async XLA Ops:
  6.5 145.7 %all-gather.3.cloned.1.call-start = ((), (), s32[]{:S(2)}) async-start(), calls=%async_computation.6 | async-start | bytes 9732096 | tf_op jit(solution)/shard_map/all_gather | solution.py:57
  7.3 282.0 %all-gather.5.cloned.1.call-start = ((), (), s32[]{:S(2)}) async-start(), calls=%async_computation.7 | async-start | bytes 9732096 | tf_op jit(solution)/shard_map/all_gather | solution.py:56
  16.2 164.0 %all-to-all-start.2 = ((bf16[1,4,3,128,1536]{4,1,2,0,3:T(4,128)(2,1)}), bf16[1,4,3,128,1536]{4,1,2,0,3:T(4,128)(2,1)}, u32[]{:S(2)}, u32[]{:S(2)}) async-start(bf16[1,4,3,128,1536]{4,1,2,0,3:T(4,128)(2,1)} %copy.445), calls=%async_computation.2 | async-start | bytes 9437184 | tf_op jit(solution)/shard_map/all_to_all | solution.py:62
  172.2 2.1 copy-start.1
  180.1 144.1 %all-to-all-start = ((bf16[1,4,3,128,1536]{4,1,2,0,3:T(4,128)(2,1)}), bf16[1,4,3,128,1536]{4,1,2,0,3:T(4,128)(2,1)}, u32[]{:S(2)}, u32[]{:S(2)}) async-start(bf16[1,4,3,128,1536]{4,1,2,0,3:T(4,128)(2,1)} %copy.427), calls=%async_computation | async-start | bytes 9437184 | tf_op jit(solution)/shard_map/all_to_all | solution.py:64
  309.2 2.2 copy-start.2
  317.2 10.7 %copy-start.19 = (s32[1,4,3,2,2]{1,4,3,2,0:T(2,128)S(1)}, s32[1,4,3,2,2]{1,4,3,2,0:T(2,128)}, u32[]{:S(2)}) copy-start(s32[1,4,3,2,2]{1,4,3,2,0:T(2,128)} %param.9) | copy-start | bytes 580
  324.2 175.4 %all-to-all-start.1 = ((bf16[1,4,3,128,1536]{4,1,2,0,3:T(4,128)(2,1)}), bf16[1,4,3,128,1536]{4,1,2,0,3:T(4,128)(2,1)}, u32[]{:S(2)}, u32[]{:S(2)}) async-start(bf16[1,4,3,128,1536]{4,1,2,0,3:T(4,128)(2,1)} %copy.431), calls=%async_computation.1 | async-start | bytes 9437184 | tf_op jit(solution)/shard_map/all_to_all | solution.py:63
  476.3 1.4 copy-start.13
  538.2 30.7 %all-to-all-start.3 = ((f32[32,1,576]{2,1,0:T(1,128)}), f32[32,1,576]{2,1,0:T(1,128)S(1)}, u32[]{:S(2)}, u32[]{:S(2)}) async-start(f32[32,1,576]{2,1,0:T(1,128)} %reshape.1496), calls=%async_computation.3 | async-start | bytes 163840 | tf_op jit(solution)/shard_map/all_to_all | solution.py:97
  560.4 2.4 copy-start
  562.8 2.2 copy-start.10
  568.9 13.4 %all-to-all-start.5 = ((f32[32,1,576]{2,1,0:T(1,128)}), f32[32,1,576]{2,1,0:T(1,128)S(1)}, u32[]{:S(2)}, u32[]{:S(2)}) async-start(f32[32,1,576]{2,1,0:T(1,128)} %reshape.1494), calls=%async_computation.5 | async-start | bytes 163840 | tf_op jit(solution)/shard_map/all_to_all | solution.py:98
  582.9 108.7 %all-to-all-start.4 = ((bf16[32,1,4,3,4,1536]{5,2,4,3,1,0:T(4,128)(2,1)}), bf16[32,1,4,3,4,1536]{5,2,4,3,1,0:T(4,128)(2,1)}, u32[]{:S(2)}, u32[]{:S(2)}) async-start(bf16[32,1,4,3,4,1536]{5,2,4,3,1,0:T(4,128)(2,1)} %fusion.63), calls=%async_computation.4 | async-start | bytes 9437184 | tf_op jit(solution)/shard_map/all_to_all | solution.py:94
  600.8 4.3 copy-start.3
  602.4 4.3 copy-start.5
  608.9 1.4 copy-start.4
  608.9 1.9 copy-start.6
  611.6 1.5 copy-start.8
  627.8 1.5 copy-start.9
  629.2 3.2 copy-start.16
  639.2 9.4 %copy-start.17 = (f32[4,128,12]{1,2,0:T(8,128)S(1)}, f32[4,128,12]{1,2,0:T(8,128)}, u32[]{:S(2)}) copy-start(f32[4,128,12]{1,2,0:T(8,128)} %fusion.8) | copy-start | bytes 73732
  639.2 9.4 %copy-start.18 = (f32[4,128,12]{1,2,0:T(8,128)S(1)}, f32[4,128,12]{1,2,0:T(8,128)}, u32[]{:S(2)}) copy-start(f32[4,128,12]{1,2,0:T(8,128)} %fusion.10) | copy-start | bytes 73732
  709.6 12.0 %copy-start.14 = (f32[4,3,128,12]{2,3,0,1:T(8,128)S(1)}, f32[4,3,128,12]{2,3,0,1:T(8,128)}, u32[]{:S(2)}) copy-start(f32[4,3,128,12]{2,3,0,1:T(8,128)} %get-tuple-element.7) | copy-start | bytes 221188
  (4 other events, 4.9 us)
Sparse Core Ops, SparseCore 0:
  10.2 141.9 all-gather.2
  155.1 134.0 all-gather.4
